TPU v7x, 512 devices: a whole 4x8x8 slice. The times are simulated.
512 devices in a mesh: tile: 64 (over y, z_lo, core), img: 8 (over z_hi, x).
Axes of the slice: x: 4, y: 8, z: 8 (z_hi: 2, z_lo: 4; z = z_hi * 4 + z_lo), core: 2. Of those that a mesh axis runs over, the one named last changes fastest.
Arguments:
- heights: float32 [64, 64, 128], P('tile'), may hold values from -1.5 to 1.5
- albedo: float32 [64, 64, 128], P('tile'), may hold values from 0.5 to 1.5
- blocks: bfloat16 [64, 8, 64, 64, 128], P('tile', 'img'), may hold values from 0 to 1
- block_params: bfloat16 [64, 8, 64, 8], P('tile', 'img'), may hold values from -1 to 2, as said below
- block_dest: int32 [64, 8, 64, 1], P('tile', 'img'), may hold values from 0 to 63; in each aligned block of 64 rows (0 to 63, 64 to 127, ..., all dimensions but the last counted through in order) at most 2 rows name the same one
Outputs:
- grad_heights: float32 [64, 64, 128], P('tile', 'img')
- grad_albedo: float32 [64, 64, 128], P('tile', 'img')
Inputs may be any that keep to these rules, and one draw needn't show every extreme that they name: `block_params`: columns 0 to 2 are a unit sun vector whose third entry lies between 0.05 and 0.43, columns 3 to 5 a unit view vector whose first two entries lie within -0.15 and 0.15, column 6 lies between 0.2 and 0.9 and column 7 between 0.5 and 2. `block_dest`: of the blocks held by one device, at most 2 lie on any one tile, and in every draw some device holds exactly 2 blocks of some tile.
All inputs are finite; a program needn't handle non-finite values.
Results may differ from a plain program's by a relative error of at most 0.0003.
Values may be sent and summed in bfloat16 or wider, within the bound.
No kernel may reach another device: no remote copies, remote signals or barrier semaphores. Data moves between devices by JAX's collectives and lax.ppermute only.
A program may use at most 64 MiB of HBM per device.

v0:
```python
import jax
import jax.numpy as jnp
from jax import lax
from jax.sharding import PartitionSpec as P

TCOLS = 8


SMOOTH = 0.0025


def shifted(value, axis, steps):
    count = lax.axis_size(axis)
    leading, last = (max(0, -steps), min(count, count - steps))
    return lax.ppermute(value, axis, [(source, source + steps) for source in range(leading, last)])


def slot_terms(slope_x, slope_y, shrink, albedo_map, bright, params, inv_count):
    params = params.astype(jnp.float32)

    def column(channel):
        return params[..., channel][..., None, None]

    sun_x, sun_y, sun_z = (column(0), column(1), column(2))
    view_x, view_y, view_z = (column(3), column(4), column(5))
    lambert_mix, exposure = (column(6), column(7))
    toward_sun = sun_z - slope_x * sun_x - slope_y * sun_y
    toward_view = view_z - slope_x * view_x - slope_y * view_y
    cos_inc = toward_sun * shrink
    cos_emit = toward_view * shrink
    smooth_root = jnp.sqrt(cos_inc * cos_inc + SMOOTH)
    lighted = 0.5 * (cos_inc + smooth_root)
    denom_sum = lighted + cos_emit
    shading = 2.0 * lambert_mix * lighted / denom_sum + (1.0 - lambert_mix) * lighted
    misfit = exposure * albedo_map * shading - bright
    scaled = exposure * misfit * inv_count
    grad_shade = scaled * albedo_map
    albedo_term = scaled * shading
    denom_square = denom_sum * denom_sum
    grad_lit = grad_shade * (2.0 * lambert_mix * cos_emit / denom_square + 1.0 - lambert_mix)
    grad_inc = grad_lit * 0.5 * (1.0 + cos_inc / smooth_root)
    grad_emit = grad_shade * (-2.0 * lambert_mix * lighted / denom_square)
    grad_shrink = grad_inc * toward_sun + grad_emit * toward_view
    grad_sun = grad_inc * shrink
    grad_view = grad_emit * shrink
    term_x = -(sun_x * grad_sun + view_x * grad_view)
    term_y = -(sun_y * grad_sun + view_y * grad_view)
    return (term_x, term_y, grad_shrink, albedo_term)


def transpose_stencil(grad_x, grad_y, tile_row, tile_col, last_row):
    half_x = 0.5 * grad_x
    half_y = 0.5 * grad_y
    spread = (
        jnp.pad(half_x, ((1, 1), (2, 0)))
        - jnp.pad(half_x, ((1, 1), (0, 2)))
        + jnp.pad(half_y, ((2, 0), (1, 1)))
        - jnp.pad(half_y, ((0, 2), (1, 1)))
    )
    interior = spread[1:-1, 1:-1]
    top_rim = spread[0, 1:-1]
    bottom_rim = spread[-1, 1:-1]
    left_rim = spread[1:-1, 0]
    right_rim = spread[1:-1, -1]
    arrived = []
    for edge_piece, offset in (
        (top_rim, -TCOLS),
        (bottom_rim, TCOLS),
        (left_rim, -1),
        (right_rim, 1),
    ):
        arrived.append(shifted(edge_piece, "tile", offset))
    from_south = jnp.where(tile_row < last_row, arrived[0], bottom_rim)
    from_north = jnp.where(tile_row > 0, arrived[1], top_rim)
    from_east = jnp.where(tile_col < TCOLS - 1, arrived[2], right_rim)
    from_west = jnp.where(tile_col > 0, arrived[3], left_rim)
    interior = interior.at[-1].add(from_south).at[0].add(from_north)
    interior = interior.at[:, -1].add(from_east).at[:, 0].add(from_west)
    return interior


def body(heights, albedo, blocks, block_params, block_dest):
    tiles_count = lax.axis_size("tile")
    groups = lax.axis_size("img")
    tile_index = lax.axis_index("tile")
    tile_row = tile_index // TCOLS
    tile_col = tile_index % TCOLS
    last_row = tiles_count // TCOLS - 1
    height = heights[0]
    albedo_map = albedo[0]
    tile_rows, tile_cols = height.shape
    fetched = []
    for edge_piece, offset in (
        (height[-1], TCOLS),
        (height[0], -TCOLS),
        (height[:, -1], 1),
        (height[:, 0], -1),
    ):
        fetched.append(shifted(edge_piece, "tile", offset))
    north_edge = jnp.where(tile_row > 0, fetched[0], height[0])
    south_edge = jnp.where(tile_row < last_row, fetched[1], height[-1])
    west_edge = jnp.where(tile_col > 0, fetched[2], height[:, 0])
    east_edge = jnp.where(tile_col < TCOLS - 1, fetched[3], height[:, -1])
    widened = jnp.concatenate([west_edge[:, None], height, east_edge[:, None]], axis=1)
    taller = jnp.concatenate([north_edge[None], height, south_edge[None]], axis=0)
    slope_x = (widened[:, 2:] - widened[:, :-2]) * 0.5
    slope_y = (taller[2:] - taller[:-2]) * 0.5
    shrink = 1.0 / jnp.sqrt(1.0 + slope_x * slope_x + slope_y * slope_y)
    block_count = block_dest.shape[2]
    capacity = max(2, (2 * block_count + tiles_count - 1) // tiles_count)
    target = block_dest.reshape(block_count)
    position = jnp.arange(block_count, dtype=jnp.int32)
    earlier = (target[:, None] == target[None, :]) & (position[None, :] < position[:, None])
    slot_index = target * capacity + jnp.sum(earlier, axis=1, dtype=jnp.int32)
    slot_table = slot_index[None, :] == jnp.arange(tiles_count * capacity, dtype=jnp.int32)[:, None]
    filled = jnp.any(slot_table, axis=1)
    source_pick = jnp.sum(jnp.where(slot_table, position[None, :], 0), axis=1)
    bright_rows = blocks.reshape(block_count, tile_rows, tile_cols)[source_pick]
    param_rows = block_params.reshape(block_count, 8)[source_pick]
    send_bright = jnp.where(filled[:, None, None], bright_rows, jnp.zeros((), jnp.bfloat16))
    send_bright = send_bright.reshape(tiles_count, capacity, tile_rows, tile_cols)
    send_params = jnp.where(filled[:, None], param_rows, jnp.zeros((), jnp.bfloat16))
    send_params = send_params.reshape(tiles_count, capacity, 8)
    inv_count = 1.0 / block_count
    bright_in = lax.all_to_all(send_bright, "tile", split_axis=0, concat_axis=0, tiled=True)
    params_in = lax.all_to_all(send_params, "tile", split_axis=0, concat_axis=0, tiled=True)
    senders = bright_in.shape[0]
    item_count = bright_in.shape[1]
    per_step = 8

    def visit_group(totals, inputs):
        bright_part, params_part = inputs
        pieces = slot_terms(
            slope_x,
            slope_y,
            shrink,
            albedo_map,
            bright_part.astype(jnp.float32),
            params_part,
            inv_count,
        )
        return (totals + jnp.stack([jnp.sum(member, axis=0) for member in pieces]), None)

    grouped_bright = bright_in.reshape(
        senders // per_step, per_step, item_count, tile_rows, tile_cols
    )
    grouped_params = params_in.reshape(senders // per_step, per_step, item_count, 8)
    totals, unused = lax.scan(
        visit_group,
        jnp.zeros((4, item_count, tile_rows, tile_cols), jnp.float32),
        (grouped_bright, grouped_params),
    )
    per_item = totals
    totals = jnp.sum(per_item, axis=1)
    shrink_cube = shrink * shrink * shrink
    grad_x = totals[0] - slope_x * shrink_cube * totals[2]
    grad_y = totals[1] - slope_y * shrink_cube * totals[2]
    albedo_grad = totals[3]
    grad_x, grad_y, albedo_grad = lax.psum((grad_x, grad_y, albedo_grad), "img")
    spread = transpose_stencil(grad_x, grad_y, tile_row, tile_col, last_row)
    row_share = tile_rows // groups
    first_row = lax.axis_index("img") * row_share
    height_grad = lax.dynamic_slice_in_dim(spread, first_row, row_share, 0)
    albedo_part = lax.dynamic_slice_in_dim(albedo_grad, first_row, row_share, 0)
    return (height_grad[None], albedo_part[None])


def solution(mesh):
    placed = (
        P("tile", None, None),
        P("tile", None, None),
        P("tile", "img", None, None, None),
        P("tile", "img", None, None),
        P("tile", "img", None, None),
    )
    return jax.shard_map(
        body,
        mesh=mesh,
        in_specs=placed,
        out_specs=(P("tile", "img", None), P("tile", "img", None)),
        check_vma=False,
    )
```

profile of v0, /device:TPU:32, one launch (start us, length us, event | category | flops | bytes accessed | tf_op | source)
XLA Modules:
  0.0 302.1 jit_solution(965612710227657913)
XLA Ops:
  11.4 13.3 %all-to-all-start = ((bf16[64,2,8]{2,1,0:T(2,128)(2,1)}), bf16[64,2,8]{2,1,0:T(2,128)(2,1)S(1)}, u32[]{:S(2)}, u32[]{:S(2)}) async-start(bf16[64,2,8]{2,1,0:T(2,128)(2,1)} %broadcast_select_fusion.1), calls=%async_computation | async-start | bytes 65536 | tf_op jit(solution)/shard_map/all_to_all | solution.py:126
  25.7 1.6 broadcast_select_fusion
  27.2 2.4 all-to-all-done
  30.3 9.6 %all-to-all-start.1 = ((bf16[64,2,64,128]{3,2,1,0:T(8,128)(2,1)}), bf16[64,2,64,128]{3,2,1,0:T(8,128)(2,1)S(1)}, u32[]{:S(2)}, u32[]{:S(2)}) async-start(bf16[64,2,64,128]{3,2,1,0:T(8,128)(2,1)} %broadcast_select_fusion), calls=%async_computation.1 | async-start | bytes 4194304 | tf_op jit(solution)/shard_map/all_to_all | solution.py:125
  39.9 2.4 collective-permute-start.2
  42.4 3.4 %collective-permute-start.3 = (f32[128]{0:T(128)S(1)}, f32[128]{0:T(128)S(1)}, u32[]{:S(2)}, u32[]{:S(2)}) collective-permute-start(f32[128]{0:T(128)S(1)} %get-tuple-element.256), channel_id=1, source_target_pairs={{0,64},{8,72},{16,80},{24,88},{32,96},{40,104},{48,112},{56,120},{... | collective-permute-start | bytes 1544 | tf_op jit(solution)/shard_map/ppermute | solution.py:15
  46.0 5.5 %collective-permute-start = (f32[64]{0:T(128)S(1)}, f32[64]{0:T(128)S(1)}, u32[]{:S(2)}, u32[]{:S(2)}) collective-permute-start(f32[64]{0:T(128)S(1)} %get-tuple-element.210), channel_id=1, source_target_pairs={{8,0},{16,8},{24,16},{32,24},{40,32},{48,40},{56,48},{64,56},{72,6... | collective-permute-start | bytes 776 | tf_op jit(solution)/shard_map/ppermute | solution.py:15
  51.5 1.9 collective-permute-start.1
  53.5 31.1 %collective-permute-done = f32[64]{0:T(128)S(1)} collective-permute-done((f32[64]{0:T(128)S(1)}, f32[64]{0:T(128)S(1)}, u32[]{:S(2)}, u32[]{:S(2)}) %collective-permute-start) | collective-permute-done | bytes 288 | tf_op jit(solution)/shard_map/ppermute | solution.py:15
  88.3 70.1 %while.17 = (s32[]{:T(128)}, f32[4,2,64,128]{3,2,1,0:T(8,128)S(1)}, bf16[8,8,2,8]{3,2,1,0:T(2,128)(2,1)}, f32[1,64,128]{2,1,0:T(8,128)S(1)}, f32[64,128]{1,0:T(8...) while((s32[]{:T(128)}, f32[4,2,64,128]{3,2,1,0:T(8,128)S(1)}, ...), condition=%wide.region_8.9_spmd.clone, body=%wide.region_3.8_spmd.clone.sunk | while | flops 10657987 | bytes 4299399 | solution.py:148
  91.0 1.8 add_multiply_fusion.2
  92.9 2.5 add_reduce_fusion.4
  99.8 1.8 add_multiply_fusion.2
  101.7 2.5 add_reduce_fusion.4
  108.6 1.8 add_multiply_fusion.2
  110.4 2.5 add_reduce_fusion.4
  117.3 1.8 add_multiply_fusion.2
  119.2 2.5 add_reduce_fusion.4
  126.1 1.8 add_multiply_fusion.2
  127.9 2.5 add_reduce_fusion.4
  134.8 1.8 add_multiply_fusion.2
  136.7 2.5 add_reduce_fusion.4
  143.6 1.8 add_multiply_fusion.2
  145.4 2.5 add_reduce_fusion.4
  152.3 1.8 add_multiply_fusion.2
  154.2 2.5 add_reduce_fusion.4
  161.1 111.8 %all-reduce.7.cloned.1.call-done = (f32[64,128]{1,0:T(8,128)}, f32[64,128]{1,0:T(8,128)}, f32[64,128]{1,0:T(8,128)}) async-done(((f32[64,128]{1,0:T(8,128)}, f32[64,128]{1,0:T(8,128)}, f32[64,128]{1,0:T(8,128)}), (f32[64,128]{1,0:T(8,128)}, f32[64,128]{1,0:T(8,128)}, f32[64,128]{1,0:T(8,128)})) %all-reduce.7.cloned.1.call-update) | async-done | bytes 98320 | tf_op jit(solution)/shard_map/psum | solution.py:159
  273.9 1.9 collective-permute-start.7
  275.9 2.4 collective-permute-start.4
  279.7 7.0 %collective-permute-start.6 = (f32[64]{0:T(128)S(1)}, f32[64]{0:T(128)S(1)}, u32[]{:S(2)}, u32[]{:S(2)}) collective-permute-start(f32[64]{0:T(128)S(1)} %get-tuple-element.209), channel_id=1, source_target_pairs={{8,0},{16,8},{24,16},{32,24},{40,32},{48,40},{56,48},{64,56},{72,6... | collective-permute-start | bytes 776 | tf_op jit(solution)/shard_map/ppermute | solution.py:15
  286.8 3.6 %collective-permute-start.5 = (f32[128]{0:T(128)S(1)}, f32[128]{0:T(128)S(1)}, u32[]{:S(2)}, u32[]{:S(2)}) collective-permute-start(f32[128]{0:T(128)S(1)} %get-tuple-element.251), channel_id=1, source_target_pairs={{0,64},{8,72},{16,80},{24,88},{32,96},{40,104},{48,112},{56,120},{... | collective-permute-start | bytes 1544 | tf_op jit(solution)/shard_map/ppermute | solution.py:15
  290.7 2.8 collective-permute-done.5
  (284 shorter events, 51.6 us)
Async XLA Ops:
  7.2 17.5 %copy-start = (bf16[1,1,64,64,128]{4,3,2,1,0:T(8,128)(2,1)S(1)}, bf16[1,1,64,64,128]{4,3,2,1,0:T(8,128)(2,1)}, u32[]{:S(2)}) copy-start(bf16[1,1,64,64,128]{4,3,2,1,0:T(8,128)(2,1)} %param.17) | copy-start | bytes 3145732
  11.4 18.3 %all-to-all-start = ((bf16[64,2,8]{2,1,0:T(2,128)(2,1)}), bf16[64,2,8]{2,1,0:T(2,128)(2,1)S(1)}, u32[]{:S(2)}, u32[]{:S(2)}) async-start(bf16[64,2,8]{2,1,0:T(2,128)(2,1)} %broadcast_select_fusion.1), calls=%async_computation | async-start | bytes 65536 | tf_op jit(solution)/shard_map/all_to_all | solution.py:126
  27.2 12.7 %copy-start.7 = (f32[1,64,128]{2,1,0:T(8,128)S(1)}, f32[1,64,128]{2,1,0:T(8,128)}, u32[]{:S(2)}) copy-start(f32[1,64,128]{2,1,0:T(8,128)} %param.15) | copy-start | bytes 98308
  27.2 61.1 %copy-start.1 = (f32[1,64,128]{2,1,0:T(8,128)S(1)}, f32[1,64,128]{2,1,0:T(8,128)}, u32[]{:S(2)}) copy-start(f32[1,64,128]{2,1,0:T(8,128)} %param.16) | copy-start | bytes 98308
  30.3 58.0 %all-to-all-start.1 = ((bf16[64,2,64,128]{3,2,1,0:T(8,128)(2,1)}), bf16[64,2,64,128]{3,2,1,0:T(8,128)(2,1)S(1)}, u32[]{:S(2)}, u32[]{:S(2)}) async-start(bf16[64,2,64,128]{3,2,1,0:T(8,128)(2,1)} %broadcast_select_fusion), calls=%async_computation.1 | async-start | bytes 4194304 | tf_op jit(solution)/shard_map/all_to_all | solution.py:125
  39.9 233.0 %all-reduce.7.cloned.1.call-start = ((), (), s32[]{:S(2)}) async-start(), calls=%async_computation.2 | async-start | bytes 196608 | tf_op jit(solution)/shard_map/psum | solution.py:159
  39.9 46.9 %collective-permute-start.2 = (f32[128]{0:T(128)S(1)}, f32[128]{0:T(128)S(1)}, u32[]{:S(2)}, u32[]{:S(2)}) collective-permute-start(f32[128]{0:T(128)S(1)} %get-tuple-element.255), channel_id=1, source_target_pairs={{64,0},{72,8},{80,16},{88,24},{96,32},{104,40},{112,48},{120,56},{... | collective-permute-start | bytes 1544 | tf_op jit(solution)/shard_map/ppermute | solution.py:15
  42.4 44.5 %collective-permute-start.3 = (f32[128]{0:T(128)S(1)}, f32[128]{0:T(128)S(1)}, u32[]{:S(2)}, u32[]{:S(2)}) collective-permute-start(f32[128]{0:T(128)S(1)} %get-tuple-element.256), channel_id=1, source_target_pairs={{0,64},{8,72},{16,80},{24,88},{32,96},{40,104},{48,112},{56,120},{... | collective-permute-start | bytes 1544 | tf_op jit(solution)/shard_map/ppermute | solution.py:15
  46.0 38.6 %collective-permute-start = (f32[64]{0:T(128)S(1)}, f32[64]{0:T(128)S(1)}, u32[]{:S(2)}, u32[]{:S(2)}) collective-permute-start(f32[64]{0:T(128)S(1)} %get-tuple-element.210), channel_id=1, source_target_pairs={{8,0},{16,8},{24,16},{32,24},{40,32},{48,40},{56,48},{64,56},{72,6... | collective-permute-start | bytes 776 | tf_op jit(solution)/shard_map/ppermute | solution.py:15
  51.5 34.5 %collective-permute-start.1 = (f32[64]{0:T(128)S(1)}, f32[64]{0:T(128)S(1)}, u32[]{:S(2)}, u32[]{:S(2)}) collective-permute-start(f32[64]{0:T(128)S(1)} %get-tuple-element.211), channel_id=1, source_target_pairs={{0,8},{8,16},{16,24},{24,32},{32,40},{40,48},{48,56},{56,64},{64,7... | collective-permute-start | bytes 776 | tf_op jit(solution)/shard_map/ppermute | solution.py:15
  90.5 2.4 copy-start.2
  90.6 2.2 copy-start.3
  99.2 2.4 copy-start.2
  99.4 2.2 copy-start.3
  99.5 2.1 copy-start.4
  108.0 2.4 copy-start.2
  108.1 2.2 copy-start.3
  108.3 2.1 copy-start.4
  116.8 2.4 copy-start.2
  116.9 2.2 copy-start.3
  125.5 2.4 copy-start.2
  125.6 2.2 copy-start.3
  134.3 2.4 copy-start.2
  134.4 2.2 copy-start.3
  143.0 2.4 copy-start.2
  143.2 2.2 copy-start.3
  151.8 2.4 copy-start.2
  151.9 2.2 copy-start.3
  273.9 12.8 %collective-permute-start.7 = (f32[64]{0:T(128)S(1)}, f32[64]{0:T(128)S(1)}, u32[]{:S(2)}, u32[]{:S(2)}) collective-permute-start(f32[64]{0:T(128)S(1)} %get-tuple-element.208), channel_id=1, source_target_pairs={{0,8},{8,16},{16,24},{24,32},{32,40},{40,48},{48,56},{56,64},{64,7... | collective-permute-start | bytes 776 | tf_op jit(solution)/shard_map/ppermute | solution.py:15
  275.9 10.8 %collective-permute-start.4 = (f32[128]{0:T(128)S(1)}, f32[128]{0:T(128)S(1)}, u32[]{:S(2)}, u32[]{:S(2)}) collective-permute-start(f32[128]{0:T(128)S(1)} %subtract_bitcast_fusion.1), channel_id=1, source_target_pairs={{64,0},{72,8},{80,16},{88,24},{96,32},{104,40},{112,48},{120,56},{... | collective-permute-start | bytes 1544 | tf_op jit(solution)/shard_map/ppermute | solution.py:15
  279.7 10.8 %collective-permute-start.6 = (f32[64]{0:T(128)S(1)}, f32[64]{0:T(128)S(1)}, u32[]{:S(2)}, u32[]{:S(2)}) collective-permute-start(f32[64]{0:T(128)S(1)} %get-tuple-element.209), channel_id=1, source_target_pairs={{8,0},{16,8},{24,16},{32,24},{40,32},{48,40},{56,48},{64,56},{72,6... | collective-permute-start | bytes 776 | tf_op jit(solution)/shard_map/ppermute | solution.py:15
  286.8 6.7 %collective-permute-start.5 = (f32[128]{0:T(128)S(1)}, f32[128]{0:T(128)S(1)}, u32[]{:S(2)}, u32[]{:S(2)}) collective-permute-start(f32[128]{0:T(128)S(1)} %get-tuple-element.251), channel_id=1, source_target_pairs={{0,64},{8,72},{16,80},{24,88},{32,96},{40,104},{48,112},{56,120},{... | collective-permute-start | bytes 1544 | tf_op jit(solution)/shard_map/ppermute | solution.py:15
  (23 other events, 44.3 us)
Sparse Core Ops, SparseCore 0:
  160.5 112.2 all-reduce.6
where the time goes:
time: 305 us; the launch traced here: 302 us
  waiting for transfers between devices  150 us (49%)
  other arithmetic  57.2 us (19%)
  starting transfers between devices  51.2 us (17%)
  local copies, waits for them, and re-layouts  29.2 us (10%)
  between operations  14.3 us (5%)
    psum x1, waiting for transfers between devices, body(): grad_x, grad_y, albedo_grad = lax.psum((grad_x, grad_y, albedo_grad), 'img')  112 us
    ppermute x8, waiting for transfers between devices, shifted(): lax.ppermute(value, axis, [(source, source + steps) for source in range(l...  35.3 us
    ppermute x8, starting transfers between devices, shifted(): lax.ppermute(value, axis, [(source, source + steps) for source in range(l...  28.3 us
    reduce_sum x8, other arithmetic, visit_group(): jnp.sum(member, axis=0)  20.2 us
    mul x8, other arithmetic, slot_terms(): grad_inc = grad_lit * 0.5 * (1.0 + cos_inc / smooth_root)  14.5 us
    all_to_all x1, starting transfers between devices, body(): lax.all_to_all(send_params, 'tile', split_axis=0, concat_axis=0, tiled=True)  13.3 us
    all_to_all x1, starting transfers between devices, body(): lax.all_to_all(send_bright, 'tile', split_axis=0, concat_axis=0, tiled=True)  9.57 us
    add x8, other arithmetic, visit_group(): totals + jnp.stack([jnp.sum(member, axis=0) for member in pieces])  7.76 us
  transfers between devices with their start and end apart: 11, of which 5 were waited for; matrix products, arithmetic and copies ran while one was open for 2% of the time, Pallas kernels for 0%

commit v1 on v0

v1 whole, which is shorter than its diff:
```python
import functools

import jax
import jax.numpy as jnp
from jax import lax
from jax.experimental import pallas as pl
from jax.experimental.pallas import tpu as pltpu
from jax.sharding import PartitionSpec as P

TCOLS = 8
SMOOTH = 0.0025
PARAMS = 8
EXTRA = 8


def shifted(value, axis, steps):
    count = lax.axis_size(axis)
    leading, last = (max(0, -steps), min(count, count - steps))
    return lax.ppermute(value, axis, [(source, source + steps) for source in range(leading, last)])


def pack_kernel(dest_ref, params_ref, blocks_ref, send_ref, count, rows):
    tiles, tile_rows = send_ref.shape[0], blocks_ref.shape[1]
    number = blocks_ref.shape[0]

    def clear(tile, carry):
        count[tile] = 0
        return carry

    lax.fori_loop(0, tiles, clear, 0)
    rows[...] = jnp.zeros_like(rows)

    def place(index, carry):
        tile = dest_ref[index]
        slot = count[tile]
        count[tile] = slot + 1
        start = pl.multiple_of(slot * tile_rows, tile_rows)
        send_ref[tile, pl.ds(start, tile_rows), :] = blocks_ref[index]
        rows[tile, pl.ds(slot, 1), :] = params_ref[pl.ds(index, 1), :]
        return carry

    lax.fori_loop(0, number, place, 0)

    def fill(tile, carry):
        for slot in (0, 1):

            @pl.when(count[tile] <= slot)
            def _():
                send_ref[tile, slot * tile_rows : (slot + 1) * tile_rows, :] = jnp.zeros(
                    (tile_rows, send_ref.shape[2]), send_ref.dtype
                )

        send_ref[tile, 2 * tile_rows :, :] = rows[tile].astype(send_ref.dtype)
        return carry

    lax.fori_loop(0, tiles, fill, 0)


def terms_kernel(params_ref, maps_ref, got_ref, out_ref):
    senders = got_ref.shape[0]
    tile_rows = maps_ref.shape[1]
    step = 16
    groups = tile_rows // 8

    def strip(index, carry):
        first = pl.multiple_of(index * step, step)
        p = maps_ref[0, pl.ds(first, step), :]
        q = maps_ref[1, pl.ds(first, step), :]
        w = maps_ref[2, pl.ds(first, step), :]
        albedo = maps_ref[3, pl.ds(first, step), :]
        pw = p * w
        qw = q * w

        def sender(source, totals):
            north, east, up, shade = totals
            for slot in (0, 1):
                base = source * (2 * PARAMS) + slot * PARAMS
                sx, sy, sz, vx, vy, vz, mix, gain = [params_ref[base + k] for k in range(PARAMS)]
                mix2 = mix * 2.0
                rest = 1.0 - mix
                bright = got_ref[source, pl.ds(pl.multiple_of(slot * tile_rows + first, step), step), :].astype(jnp.float32)
                ci = sz * w - sx * pw - sy * qw
                ce = vz * w - vx * pw - vy * qw
                square = ci * ci + SMOOTH
                inv_root = lax.rsqrt(square)
                mu = (ci + square * inv_root) * 0.5
                inv = 1.0 / (mu + ce)
                k = mix2 * inv
                u = mu * inv
                c = ce * inv
                shading = mu * (k + rest)
                misfit = (gain * albedo) * shading - bright
                scaled = gain * misfit
                shade = shade + scaled * shading
                gs = scaled * albedo
                gk = gs * k
                gl = gk * c + gs * rest
                gi = gl * (mu * inv_root)
                ge = gk * u
                north = north + (gi * sx - ge * vx)
                east = east + (gi * sy - ge * vy)
                up = up + (gi * sz - ge * vz)
            return (north, east, up, shade)

        zero = jnp.zeros((step, maps_ref.shape[2]), jnp.float32)
        nx, ny, nz, shade = lax.fori_loop(0, senders, sender, (zero, zero, zero, zero), unroll=2)
        up = nz - p * nx - q * ny
        cube = w * w * w
        scale = 1.0 / 64.0
        gx = (-(w * nx) - p * cube * up) * scale
        gy = (-(w * ny) - q * cube * up) * scale
        shade = shade * scale
        for half in (0, 1):
            group = index * 2 + half
            part = slice(half * 8, half * 8 + 8)
            out_ref[group, 0:8, :] = gx[part]
            out_ref[group, 8:16, :] = gy[part]
            out_ref[group, 16:24, :] = shade[part]
        return carry

    lax.fori_loop(0, tile_rows // step, strip, 0)


def body(heights, albedo, blocks, block_params, block_dest):
    tiles_count = lax.axis_size("tile")
    groups = lax.axis_size("img")
    tile_index = lax.axis_index("tile")
    group = lax.axis_index("img")
    tile_row = tile_index // TCOLS
    tile_col = tile_index % TCOLS
    last_row = tiles_count // TCOLS - 1
    height = heights[0]
    albedo_map = albedo[0]
    tile_rows, tile_cols = height.shape
    block_count = block_dest.shape[2]

    params_wide = jnp.pad(
        block_params.reshape(block_count, PARAMS).astype(jnp.float32), ((0, 0), (0, tile_cols - PARAMS))
    )
    message = 2 * tile_rows + EXTRA
    send = pl.pallas_call(
        pack_kernel,
        out_shape=jax.ShapeDtypeStruct((tiles_count, message, tile_cols), jnp.bfloat16),
        in_specs=[
            pl.BlockSpec(memory_space=pltpu.SMEM),
            pl.BlockSpec(memory_space=pltpu.VMEM),
            pl.BlockSpec(memory_space=pltpu.VMEM),
        ],
        out_specs=pl.BlockSpec(memory_space=pltpu.VMEM),
        scratch_shapes=[
            pltpu.SMEM((tiles_count,), jnp.int32),
            pltpu.VMEM((tiles_count, EXTRA, tile_cols), jnp.float32),
        ],
        name="pack",
    )(block_dest.reshape(block_count), params_wide, blocks.reshape(block_count, tile_rows, tile_cols))
    got = lax.all_to_all(send, "tile", split_axis=0, concat_axis=0, tiled=True)

    fetched = []
    for edge_piece, offset in (
        (height[-1], TCOLS),
        (height[0], -TCOLS),
        (height[:, -1], 1),
        (height[:, 0], -1),
    ):
        fetched.append(shifted(edge_piece, "tile", offset))
    north_edge = jnp.where(tile_row > 0, fetched[0], height[0])
    south_edge = jnp.where(tile_row < last_row, fetched[1], height[-1])
    west_edge = jnp.where(tile_col > 0, fetched[2], height[:, 0])
    east_edge = jnp.where(tile_col < TCOLS - 1, fetched[3], height[:, -1])
    widened = jnp.concatenate([west_edge[:, None], height, east_edge[:, None]], axis=1)
    taller = jnp.concatenate([north_edge[None], height, south_edge[None]], axis=0)
    slope_x = (widened[:, 2:] - widened[:, :-2]) * 0.5
    slope_y = (taller[2:] - taller[:-2]) * 0.5
    shrink = 1.0 / jnp.sqrt(1.0 + slope_x * slope_x + slope_y * slope_y)
    maps = jnp.stack([slope_x, slope_y, shrink, albedo_map])

    params_in = got[:, 2 * tile_rows : 2 * tile_rows + 2, :PARAMS].astype(jnp.float32).reshape(-1)
    parts = pl.pallas_call(
        terms_kernel,
        out_shape=jax.ShapeDtypeStruct((groups, 24, tile_cols), jnp.float32),
        in_specs=[
            pl.BlockSpec(memory_space=pltpu.SMEM),
            pl.BlockSpec(memory_space=pltpu.VMEM),
            pl.BlockSpec(memory_space=pltpu.VMEM),
        ],
        out_specs=pl.BlockSpec(memory_space=pltpu.VMEM),
        name="terms",
    )(params_in, maps, got)

    summed = jnp.sum(lax.all_to_all(parts, "img", split_axis=0, concat_axis=0, tiled=True), axis=0)
    grad_x, grad_y, grad_albedo = (summed[0:8], summed[8:16], summed[16:24])

    def strip_shift(value, steps):
        axes = ("tile", "img")
        pairs = []
        for source in range(tiles_count * groups):
            tile, part = divmod(source, groups)
            row, col = divmod(tile, TCOLS)
            strip = row * groups + part + steps
            if 0 <= strip < (tiles_count // TCOLS) * groups:
                pairs.append((source, ((strip // groups) * TCOLS + col) * groups + strip % groups))
        return lax.ppermute(value, axes, pairs)

    from_north = strip_shift(grad_y[-1], 1)
    from_south = strip_shift(grad_y[0], -1)
    columns = tile_col
    east_pairs = [(t, t + 1) for t in range(tiles_count) if t % TCOLS < TCOLS - 1]
    from_west = lax.ppermute(grad_x[:, -1], "tile", east_pairs)
    from_east = lax.ppermute(grad_x[:, 0], "tile", [(b, a) for a, b in east_pairs])
    top = (tile_row == 0) & (group == 0)
    bottom = (tile_row == last_row) & (group == groups - 1)
    above = jnp.where(top, -grad_y[0], from_north)
    below = jnp.where(bottom, -grad_y[-1], from_south)
    before = jnp.where(columns == 0, -grad_x[:, 0], from_west)
    after = jnp.where(columns == TCOLS - 1, -grad_x[:, -1], from_east)
    wide = jnp.concatenate([before[:, None], grad_x, after[:, None]], axis=1)
    tall = jnp.concatenate([above[None], grad_y, below[None]], axis=0)
    grad_heights = 0.5 * (wide[:, :-2] - wide[:, 2:] + tall[:-2] - tall[2:])
    return (grad_heights[None], grad_albedo[None])


def solution(mesh):
    placed = (
        P("tile", None, None),
        P("tile", None, None),
        P("tile", "img", None, None, None),
        P("tile", "img", None, None),
        P("tile", "img", None, None),
    )
    return jax.shard_map(
        body,
        mesh=mesh,
        in_specs=placed,
        out_specs=(P("tile", "img", None), P("tile", "img", None)),
        check_vma=False,
    )
```

time: 305 us -> 129 us (0.42)
  the two profiles are of different devices: /device:TPU:32 before, /device:TPU:9 now
where the time goes in v1:
time: 129 us; the launch traced here: 128 us
  starting transfers between devices  53.6 us (42%)
  waiting for transfers between devices  51.5 us (40%)
  Pallas kernels  17 us (13%)
  local copies, waits for them, and re-layouts  3.45 us (3%)
  other arithmetic  2.1 us (2%)
    ppermute x4, waiting for transfers between devices, shifted(): lax.ppermute(value, axis, [(source, source + steps) for source in range(l...  36.4 us
    all_to_all x1, starting transfers between devices, body(): got = lax.all_to_all(send, 'tile', split_axis=0, concat_axis=0, tiled=True)  13.9 us
    ppermute x2, starting transfers between devices, strip_shift(): return lax.ppermute(value, axes, pairs)  12.2 us
    pallas_call x1, Pallas kernels, body(): pl.pallas_call(terms_kernel, out_shape=jax.ShapeDtypeStruct((groups, 24,...  11.7 us
    ppermute x4, starting transfers between devices, shifted(): lax.ppermute(value, axis, [(source, source + steps) for source in range(l...  10.6 us
    all_to_all x1, starting transfers between devices, body(): lax.all_to_all(parts, 'img', split_axis=0, concat_axis=0, tiled=True)  9.77 us
    all_to_all x1, waiting for transfers between devices, body(): lax.all_to_all(parts, 'img', split_axis=0, concat_axis=0, tiled=True)  9.25 us
    pallas_call x1, Pallas kernels, body(): pl.pallas_call(pack_kernel, out_shape=jax.ShapeDtypeStruct((tiles_count,...  5.29 us
  transfers between devices with their start and end apart: 10, of which 6 were waited for; matrix products, arithmetic and copies ran while one was open for 1% of the time, Pallas kernels for 0%

profile of v1, /device:TPU:9, one launch (start us, length us, event | category | flops | bytes accessed | tf_op | source)
XLA Modules:
  0.0 128.4 jit_solution(14349845723300906201)
XLA Ops:
  0.6 0.8 copy.12
  1.4 0.6 pad_convert_fusion.params_ref
  2.0 5.3 %pack.1 = bf16[64,136,128]{2,1,0:T(8,128)(2,1)} custom-call(s32[64]{0:T(128)} %bitcast.50, f32[64,128]{1,0:T(8,128)} %pad_convert_fusion.params_ref, bf16[64,64,128]{2,1,0:T(8,128)(2,1)} %bitcast.46), custom_call_target="tpu_custom_call" | custom-call | tf_op jit(solution)/shard_map/pack/pallas_call | solution.py:141
  7.3 13.9 %all-to-all-start = ((bf16[64,136,128]{2,1,0:T(8,128)(2,1)}), bf16[64,136,128]{2,1,0:T(8,128)(2,1)S(1)}, u32[]{:S(2)}, u32[]{:S(2)}) async-start(bf16[64,136,128]{2,1,0:T(8,128)(2,1)} %pack.1), calls=%async_computation | async-start | bytes 4456448 | tf_op jit(solution)/shard_map/all_to_all | solution.py:156
  21.3 0.2 slice_reduce_fusion.1
  21.5 3.4 %collective-permute-start.1 = (f32[64]{0:T(128)S(1)}, f32[64]{0:T(128)S(1)}, u32[]{:S(2)}, u32[]{:S(2)}) collective-permute-start(f32[64]{0:T(128)S(1)} %get-tuple-element.3), channel_id=1, source_target_pairs={{0,8},{8,16},{16,24},{24,32},{32,40},{40,48},{48,56},{56,64},{64,7... | collective-permute-start | bytes 776 | tf_op jit(solution)/shard_map/ppermute | solution.py:19
  24.8 1.9 %collective-permute-start = (f32[64]{0:T(128)S(1)}, f32[64]{0:T(128)S(1)}, u32[]{:S(2)}, u32[]{:S(2)}) collective-permute-start(f32[64]{0:T(128)S(1)} %get-tuple-element.2), channel_id=1, source_target_pairs={{8,0},{16,8},{24,16},{32,24},{40,32},{48,40},{56,48},{64,56},{72,6... | collective-permute-start | bytes 776 | tf_op jit(solution)/shard_map/ppermute | solution.py:19
  26.8 2.2 %collective-permute-start.2 = (f32[128]{0:T(128)S(1)}, f32[128]{0:T(128)S(1)}, u32[]{:S(2)}, u32[]{:S(2)}) collective-permute-start(f32[128]{0:T(128)S(1)} %get-tuple-element.11), channel_id=1, source_target_pairs={{64,0},{72,8},{80,16},{88,24},{96,32},{104,40},{112,48},{120,56},{... | collective-permute-start | bytes 1544 | tf_op jit(solution)/shard_map/ppermute | solution.py:19
  29.0 3.1 %collective-permute-start.3 = (f32[128]{0:T(128)S(1)}, f32[128]{0:T(128)S(1)}, u32[]{:S(2)}, u32[]{:S(2)}) collective-permute-start(f32[128]{0:T(128)S(1)} %get-tuple-element.12), channel_id=1, source_target_pairs={{0,64},{8,72},{16,80},{24,88},{32,96},{40,104},{48,112},{56,120},{... | collective-permute-start | bytes 1544 | tf_op jit(solution)/shard_map/ppermute | solution.py:19
  32.1 24.5 %collective-permute-done.1 = f32[64]{0:T(128)S(1)} collective-permute-done((f32[64]{0:T(128)S(1)}, f32[64]{0:T(128)S(1)}, u32[]{:S(2)}, u32[]{:S(2)}) %collective-permute-start.1) | collective-permute-done | bytes 288 | tf_op jit(solution)/shard_map/ppermute | solution.py:19
  56.6 0.1 copy.14
  56.7 0.1 copy.13
  56.8 11.5 %collective-permute-done.2 = f32[128]{0:T(128)S(1)} collective-permute-done((f32[128]{0:T(128)S(1)}, f32[128]{0:T(128)S(1)}, u32[]{:S(2)}, u32[]{:S(2)}) %collective-permute-start.2) | collective-permute-done | bytes 544 | tf_op jit(solution)/shard_map/ppermute | solution.py:19
  68.4 0.4 collective-permute-done.3
  68.7 0.1 fusion.10
  68.9 0.7 pad_maximum_fusion.maps_ref
  69.5 5.1 %all-to-all-done.got_ref = bf16[64,136,128]{2,1,0:T(8,128)(2,1)S(1)} async-done(((bf16[64,136,128]{2,1,0:T(8,128)(2,1)}), bf16[64,136,128]{2,1,0:T(8,128)(2,1)S(1)}, u32[]{:S(2)}, u32[]{:S(2)}) %all-to-all-start) | async-done | bytes 2228256 | tf_op jit(solution)/shard_map/all_to_all | solution.py:156
  74.6 0.9 reshape.27.params_ref
  75.5 0.5 copy-done
  76.0 11.7 %terms.1 = f32[8,24,128]{2,1,0:T(8,128)} custom-call(f32[1024]{0:T(1024)} %reshape.27.params_ref, f32[4,64,128]{2,1,0:T(8,128)} %pad_maximum_fusion.maps_ref, bf16[64,136,128]{2,1,0:T(8,128)(2,1)} %copy-done), custom_call_target="tpu_custom_call" | custom-call | tf_op jit(solution)/shard_map/terms/pallas_call | solution.py:178
  87.7 9.8 %all-to-all-start.1 = ((f32[8,24,128]{2,1,0:T(8,128)}), f32[8,24,128]{2,1,0:T(8,128)S(1)}, u32[]{:S(2)}, u32[]{:S(2)}) async-start(f32[8,24,128]{2,1,0:T(8,128)} %terms.1), calls=%async_computation.1 | async-start | bytes 196608 | tf_op jit(solution)/shard_map/all_to_all | solution.py:190
  97.5 9.3 %all-to-all-done.1 = f32[8,24,128]{2,1,0:T(8,128)S(1)} async-done(((f32[8,24,128]{2,1,0:T(8,128)}), f32[8,24,128]{2,1,0:T(8,128)S(1)}, u32[]{:S(2)}, u32[]{:S(2)}) %all-to-all-start.1) | async-done | bytes 98336 | tf_op jit(solution)/shard_map/all_to_all | solution.py:190
  106.7 0.6 slice_bitcast_fusion
  107.3 0.2 slice_reduce_fusion.2
  107.5 2.2 %collective-permute-start.6 = (f32[128]{0:T(128)S(1)}, f32[128]{0:T(128)S(1)}, u32[]{:S(2)}, u32[]{:S(2)}) collective-permute-start(f32[128]{0:T(128)S(1)} %get-tuple-element.18), channel_id=1, source_target_pairs={{0,1},{1,2},{2,3},{3,4},{4,5},{5,6},{6,7},{7,64},{8,9},{9,10},{10,... | collective-permute-start | bytes 1544 | tf_op jit(solution)/shard_map/ppermute | solution.py:202
  109.7 10.0 %collective-permute-start.7 = (f32[128]{0:T(128)S(1)}, f32[128]{0:T(128)S(1)}, u32[]{:S(2)}, u32[]{:S(2)}) collective-permute-start(f32[128]{0:T(128)S(1)} %get-tuple-element.19), channel_id=1, source_target_pairs={{1,0},{2,1},{3,2},{4,3},{5,4},{6,5},{7,6},{9,8},{10,9},{11,10},{12... | collective-permute-start | bytes 1544 | tf_op jit(solution)/shard_map/ppermute | solution.py:202
  119.7 4.1 %collective-permute-start.5 = (f32[8]{0:T(128)S(1)}, f32[8]{0:T(128)S(1)}, u32[]{:S(2)}, u32[]{:S(2)}) collective-permute-start(f32[8]{0:T(128)S(1)} %get-tuple-element.5), channel_id=1, source_target_pairs={{8,0},{16,8},{24,16},{32,24},{40,32},{48,40},{56,48},{72,64},{80,7... | collective-permute-start | bytes 104 | tf_op jit(solution)/shard_map/ppermute | solution.py:209
  123.8 3.0 %collective-permute-start.4 = (f32[8]{0:T(128)S(1)}, f32[8]{0:T(128)S(1)}, u32[]{:S(2)}, u32[]{:S(2)}) collective-permute-start(f32[8]{0:T(128)S(1)} %get-tuple-element.4), channel_id=1, source_target_pairs={{0,8},{8,16},{16,24},{24,32},{32,40},{40,48},{48,56},{64,72},{72,8... | collective-permute-start | bytes 104 | tf_op jit(solution)/shard_map/ppermute | solution.py:208
  126.9 0.7 collective-permute-done.4
  127.5 0.1 copy.16
  127.6 0.1 copy.15
  127.7 0.7 fusion.7
  (19 shorter events, 0.1 us)
Async XLA Ops:
  7.3 14.0 %copy-start.1 = (f32[1,64,128]{2,1,0:T(8,128)S(1)}, f32[1,64,128]{2,1,0:T(8,128)}, u32[]{:S(2)}) copy-start(f32[1,64,128]{2,1,0:T(8,128)} %param.5) | copy-start | bytes 98308
  7.3 61.5 %copy-start.2 = (f32[1,64,128]{2,1,0:T(8,128)S(1)}, f32[1,64,128]{2,1,0:T(8,128)}, u32[]{:S(2)}) copy-start(f32[1,64,128]{2,1,0:T(8,128)} %param.6) | copy-start | bytes 98308
  7.3 67.3 %all-to-all-start = ((bf16[64,136,128]{2,1,0:T(8,128)(2,1)}), bf16[64,136,128]{2,1,0:T(8,128)(2,1)S(1)}, u32[]{:S(2)}, u32[]{:S(2)}) async-start(bf16[64,136,128]{2,1,0:T(8,128)(2,1)} %pack.1), calls=%async_computation | async-start | bytes 4456448 | tf_op jit(solution)/shard_map/all_to_all | solution.py:156
  21.5 35.2 %collective-permute-start.1 = (f32[64]{0:T(128)S(1)}, f32[64]{0:T(128)S(1)}, u32[]{:S(2)}, u32[]{:S(2)}) collective-permute-start(f32[64]{0:T(128)S(1)} %get-tuple-element.3), channel_id=1, source_target_pairs={{0,8},{8,16},{16,24},{24,32},{32,40},{40,48},{48,56},{56,64},{64,7... | collective-permute-start | bytes 776 | tf_op jit(solution)/shard_map/ppermute | solution.py:19
  24.8 31.8 %collective-permute-start = (f32[64]{0:T(128)S(1)}, f32[64]{0:T(128)S(1)}, u32[]{:S(2)}, u32[]{:S(2)}) collective-permute-start(f32[64]{0:T(128)S(1)} %get-tuple-element.2), channel_id=1, source_target_pairs={{8,0},{16,8},{24,16},{32,24},{40,32},{48,40},{56,48},{64,56},{72,6... | collective-permute-start | bytes 776 | tf_op jit(solution)/shard_map/ppermute | solution.py:19
  26.8 41.6 %collective-permute-start.2 = (f32[128]{0:T(128)S(1)}, f32[128]{0:T(128)S(1)}, u32[]{:S(2)}, u32[]{:S(2)}) collective-permute-start(f32[128]{0:T(128)S(1)} %get-tuple-element.11), channel_id=1, source_target_pairs={{64,0},{72,8},{80,16},{88,24},{96,32},{104,40},{112,48},{120,56},{... | collective-permute-start | bytes 1544 | tf_op jit(solution)/shard_map/ppermute | solution.py:19
  29.0 39.8 %collective-permute-start.3 = (f32[128]{0:T(128)S(1)}, f32[128]{0:T(128)S(1)}, u32[]{:S(2)}, u32[]{:S(2)}) collective-permute-start(f32[128]{0:T(128)S(1)} %get-tuple-element.12), channel_id=1, source_target_pairs={{0,64},{8,72},{16,80},{24,88},{32,96},{40,104},{48,112},{56,120},{... | collective-permute-start | bytes 1544 | tf_op jit(solution)/shard_map/ppermute | solution.py:19
  74.6 1.4 %copy-start = (bf16[64,136,128]{2,1,0:T(8,128)(2,1)}, bf16[64,136,128]{2,1,0:T(8,128)(2,1)S(1)}, u32[]{:S(2)}) copy-start(bf16[64,136,128]{2,1,0:T(8,128)(2,1)S(1)} %all-to-all-done.got_ref) | copy-start | bytes 6684676
  87.7 19.0 %all-to-all-start.1 = ((f32[8,24,128]{2,1,0:T(8,128)}), f32[8,24,128]{2,1,0:T(8,128)S(1)}, u32[]{:S(2)}, u32[]{:S(2)}) async-start(f32[8,24,128]{2,1,0:T(8,128)} %terms.1), calls=%async_computation.1 | async-start | bytes 196608 | tf_op jit(solution)/shard_map/all_to_all | solution.py:190
  107.5 20.2 %collective-permute-start.6 = (f32[128]{0:T(128)S(1)}, f32[128]{0:T(128)S(1)}, u32[]{:S(2)}, u32[]{:S(2)}) collective-permute-start(f32[128]{0:T(128)S(1)} %get-tuple-element.18), channel_id=1, source_target_pairs={{0,1},{1,2},{2,3},{3,4},{4,5},{5,6},{6,7},{7,64},{8,9},{9,10},{10,... | collective-permute-start | bytes 1544 | tf_op jit(solution)/shard_map/ppermute | solution.py:202
  109.7 18.0 %collective-permute-start.7 = (f32[128]{0:T(128)S(1)}, f32[128]{0:T(128)S(1)}, u32[]{:S(2)}, u32[]{:S(2)}) collective-permute-start(f32[128]{0:T(128)S(1)} %get-tuple-element.19), channel_id=1, source_target_pairs={{1,0},{2,1},{3,2},{4,3},{5,4},{6,5},{7,6},{9,8},{10,9},{11,10},{12... | collective-permute-start | bytes 1544 | tf_op jit(solution)/shard_map/ppermute | solution.py:202
  119.7 7.1 %collective-permute-start.5 = (f32[8]{0:T(128)S(1)}, f32[8]{0:T(128)S(1)}, u32[]{:S(2)}, u32[]{:S(2)}) collective-permute-start(f32[8]{0:T(128)S(1)} %get-tuple-element.5), channel_id=1, source_target_pairs={{8,0},{16,8},{24,16},{32,24},{40,32},{48,40},{56,48},{72,64},{80,7... | collective-permute-start | bytes 104 | tf_op jit(solution)/shard_map/ppermute | solution.py:209
  123.8 3.7 %collective-permute-start.4 = (f32[8]{0:T(128)S(1)}, f32[8]{0:T(128)S(1)}, u32[]{:S(2)}, u32[]{:S(2)}) collective-permute-start(f32[8]{0:T(128)S(1)} %get-tuple-element.4), channel_id=1, source_target_pairs={{0,8},{8,16},{16,24},{24,32},{32,40},{40,48},{48,56},{64,72},{72,8... | collective-permute-start | bytes 104 | tf_op jit(solution)/shard_map/ppermute | solution.py:208

commit v2 on v0

v2 whole, which is shorter than its diff:
```python
import jax
import jax.numpy as jnp
from jax import lax
from jax.experimental import pallas as pl
from jax.experimental.pallas import tpu as pltpu
from jax.sharding import PartitionSpec as P

TCOLS = 8
SMOOTH = 0.0025
PARAMS = 8
EXTRA = 8
STRIP = 16

SMEM = pl.BlockSpec(memory_space=pltpu.SMEM)
VMEM = pl.BlockSpec(memory_space=pltpu.VMEM)


def tile_shift(value, rows, cols):
    count = lax.axis_size("tile")
    pairs = []
    for source in range(count):
        row, col = divmod(source, TCOLS)
        if 0 <= row + rows < count // TCOLS and 0 <= col + cols < TCOLS:
            pairs.append((source, source + rows * TCOLS + cols))
    return lax.ppermute(value, "tile", pairs)


def fill_table(dest_ref, table):
    number = dest_ref.shape[0]

    def clear(index, carry):
        table[index] = -1
        return carry

    lax.fori_loop(0, table.shape[0], clear, 0, unroll=8)

    def note(index, carry):
        place = dest_ref[index] * 2
        second = (table[place] >= 0).astype(jnp.int32)
        table[place + second] = index
        return carry

    lax.fori_loop(0, number, note, 0, unroll=4)


def pack_kernel(dest_ref, params_ref, blocks_ref, send_ref, table, near, far):
    tile_rows = blocks_ref.shape[1]
    fill_table(dest_ref, table)
    near[...] = params_ref[...]
    far[...] = pltpu.roll(params_ref[...], PARAMS, 1)

    def place(tile, carry):
        line = jnp.zeros((1, near.shape[1]), jnp.float32)
        for slot, rows in ((0, near), (1, far)):
            block = table[2 * tile + slot]
            kept = block >= 0
            block = jnp.maximum(block, 0)
            values = blocks_ref[block]
            send_ref[tile, slot * tile_rows : (slot + 1) * tile_rows, :] = jnp.where(kept, values, jnp.zeros_like(values))
            line = line + jnp.where(kept, rows[pl.ds(block, 1), :], 0.0)
        send_ref[tile, 2 * tile_rows :, :] = jnp.broadcast_to(line, (EXTRA, line.shape[1])).astype(send_ref.dtype)
        return carry

    lax.fori_loop(0, send_ref.shape[0], place, 0, unroll=2)


def pack(tiles, dest, params_wide, blocks):
    number, tile_rows, tile_cols = blocks.shape
    return pl.pallas_call(
        pack_kernel,
        out_shape=jax.ShapeDtypeStruct((tiles, 2 * tile_rows + EXTRA, tile_cols), jnp.bfloat16),
        in_specs=[SMEM, VMEM, VMEM],
        out_specs=VMEM,
        scratch_shapes=[pltpu.SMEM((2 * tiles,), jnp.int32)] + [pltpu.VMEM(params_wide.shape, jnp.float32)] * 2,
        name="pack",
    )(dest, params_wide, blocks)


def add_terms(params_ref, maps_ref, got_ref, first):
    tile_rows = maps_ref.shape[1]
    p = maps_ref[0, pl.ds(first, STRIP), :]
    q = maps_ref[1, pl.ds(first, STRIP), :]
    w = maps_ref[2, pl.ds(first, STRIP), :]
    albedo = maps_ref[3, pl.ds(first, STRIP), :]
    pw = p * w
    qw = q * w

    def sender(source, totals):
        sum_x, sum_y, sum_z, shade = totals
        for slot in (0, 1):
            base = source * (2 * PARAMS) + slot * PARAMS
            sx, sy, sz, vx, vy, vz, mix, gain = [params_ref[base + k] for k in range(PARAMS)]
            mix2 = mix * 2.0
            rest = 1.0 - mix
            bright = got_ref[source, pl.ds(pl.multiple_of(slot * tile_rows + first, STRIP), STRIP), :].astype(jnp.float32)
            ci = sz * w - sx * pw - sy * qw
            ce = vz * w - vx * pw - vy * qw
            square = ci * ci + SMOOTH
            inv_root = lax.rsqrt(square)
            mu = (ci + square * inv_root) * 0.5
            inv = 1.0 / (mu + ce)
            k = mix2 * inv
            u = mu * inv
            c = ce * inv
            shading = mu * (k + rest)
            misfit = (gain * albedo) * shading - bright
            scaled = gain * misfit
            shade = shade + scaled * shading
            gs = scaled * albedo
            gk = gs * k
            gl = gk * c + gs * rest
            gi = gl * (mu * inv_root)
            ge = gk * u
            sum_x = sum_x + (gi * sx - ge * vx)
            sum_y = sum_y + (gi * sy - ge * vy)
            sum_z = sum_z + (gi * sz - ge * vz)
        return (sum_x, sum_y, sum_z, shade)

    zero = jnp.zeros((STRIP, maps_ref.shape[2]), jnp.float32)
    return lax.fori_loop(0, got_ref.shape[0], sender, (zero,) * 4, unroll=2)


def terms_kernel(scale, params_ref, maps_ref, got_ref, out_ref):
    def strip(index, carry):
        first = pl.multiple_of(index * STRIP, STRIP)
        part = pl.ds(first, STRIP)
        nx, ny, nz, shade = add_terms(params_ref, maps_ref, got_ref, first)
        p, q, w = (maps_ref[k, part, :] for k in range(3))
        up = (w * w * w) * (nz - p * nx - q * ny)
        out_ref[0, part, :] = (-(w * nx) - p * up) * (0.5 * scale)
        out_ref[1, part, :] = (-(w * ny) - q * up) * (0.5 * scale)
        out_ref[2, part, :] = shade * scale
        return carry

    lax.fori_loop(0, maps_ref.shape[1] // STRIP, strip, 0)


def body(heights, albedo, blocks, block_params, block_dest):
    tiles_count = lax.axis_size("tile")
    groups = lax.axis_size("img")
    tile_index = lax.axis_index("tile")
    tile_row = tile_index // TCOLS
    tile_col = tile_index % TCOLS
    last_row = tiles_count // TCOLS - 1
    last_col = TCOLS - 1
    height = heights[0]
    albedo_map = albedo[0]
    tile_rows, tile_cols = height.shape
    block_count = block_dest.shape[2]

    params_wide = jnp.pad(
        block_params.reshape(block_count, PARAMS).astype(jnp.float32), ((0, 0), (0, tile_cols - PARAMS))
    )
    dest = block_dest.reshape(block_count)
    images = blocks.reshape(block_count, tile_rows, tile_cols)
    send = pack(tiles_count, dest, params_wide, images)
    got = lax.all_to_all(send, "tile", split_axis=0, concat_axis=0, tiled=True)

    north_edge = jnp.where(tile_row > 0, tile_shift(height[-1], 1, 0), height[0])
    south_edge = jnp.where(tile_row < last_row, tile_shift(height[0], -1, 0), height[-1])
    west_edge = jnp.where(tile_col > 0, tile_shift(height[:, -1], 0, 1), height[:, 0])
    east_edge = jnp.where(tile_col < last_col, tile_shift(height[:, 0], 0, -1), height[:, -1])
    widened = jnp.concatenate([west_edge[:, None], height, east_edge[:, None]], axis=1)
    taller = jnp.concatenate([north_edge[None], height, south_edge[None]], axis=0)
    slope_x = (widened[:, 2:] - widened[:, :-2]) * 0.5
    slope_y = (taller[2:] - taller[:-2]) * 0.5
    shrink = 1.0 / jnp.sqrt(1.0 + slope_x * slope_x + slope_y * slope_y)
    maps = jnp.stack([slope_x, slope_y, shrink, albedo_map])

    params_in = got[:, 2 * tile_rows, : 2 * PARAMS].astype(jnp.float32).reshape(-1)
    half_x, half_y, albedo_grad = pl.pallas_call(
        lambda *refs: terms_kernel(1.0 / block_count, *refs),
        out_shape=jax.ShapeDtypeStruct((3, tile_rows, tile_cols), jnp.float32),
        in_specs=[SMEM, VMEM, VMEM],
        out_specs=VMEM,
        name="terms",
    )(params_in, maps, got)

    from_north = tile_shift(half_y[-1], 1, 0)
    from_south = tile_shift(half_y[0], -1, 0)
    from_west = tile_shift(half_x[:, -1], 0, 1)
    from_east = tile_shift(half_x[:, 0], 0, -1)
    above = jnp.where(tile_row == 0, -half_y[0], from_north)
    below = jnp.where(tile_row == last_row, -half_y[-1], from_south)
    before = jnp.where(tile_col == 0, -half_x[:, 0], from_west)
    after = jnp.where(tile_col == last_col, -half_x[:, -1], from_east)
    wide = jnp.concatenate([before[:, None], half_x, after[:, None]], axis=1)
    tall = jnp.concatenate([above[None], half_y, below[None]], axis=0)
    height_grad = wide[:, :-2] - wide[:, 2:] + tall[:-2] - tall[2:]
    both = jnp.stack([height_grad, albedo_grad]).reshape(2, groups, tile_rows // groups, tile_cols)
    swapped = lax.all_to_all(both.swapaxes(0, 1), "img", split_axis=0, concat_axis=0, tiled=True)
    summed = jnp.sum(swapped, axis=0)
    return (summed[:1], summed[1:])


def solution(mesh):
    placed = (
        P("tile", None, None),
        P("tile", None, None),
        P("tile", "img", None, None, None),
        P("tile", "img", None, None),
        P("tile", "img", None, None),
    )
    return jax.shard_map(
        body,
        mesh=mesh,
        in_specs=placed,
        out_specs=(P("tile", "img", None), P("tile", "img", None)),
        check_vma=False,
    )
```

time: 305 us -> 123 us (0.40)
  the two profiles are of different devices: /device:TPU:32 before, /device:TPU:72 now
where the time goes in v2:
time: 123 us; the launch traced here: 122 us
  waiting for transfers between devices  43.5 us (35%)
  starting transfers between devices  34.2 us (28%)
  blocking collectives  20.1 us (16%)
  Pallas kernels  16 us (13%)
  local copies, waits for them, and re-layouts  4.88 us (4%)
  other arithmetic  2.28 us (2%)
    ppermute x8, waiting for transfers between devices, tile_shift(): return lax.ppermute(value, 'tile', pairs)  39.2 us
    ppermute x8, starting transfers between devices, tile_shift(): return lax.ppermute(value, 'tile', pairs)  21.5 us
    all_to_all x1, blocking collectives, body(): lax.all_to_all(both.swapaxes(0, 1), 'img', split_axis=0, concat_axis=0, t...  20.1 us
    all_to_all x1, starting transfers between devices, body(): got = lax.all_to_all(send, 'tile', split_axis=0, concat_axis=0, tiled=True)  12.8 us
    pallas_call x1, Pallas kernels, body(): pl.pallas_call(lambda *refs: terms_kernel(1.0 / block_count, *refs), out_...  11.8 us
    all_to_all x1, waiting for transfers between devices, body(): got = lax.all_to_all(send, 'tile', split_axis=0, concat_axis=0, tiled=True)  4.27 us
    pallas_call x1, Pallas kernels, pack(): pl.pallas_call(pack_kernel, out_shape=jax.ShapeDtypeStruct((tiles, 2 * ti...  4.23 us
  transfers between devices with their start and end apart: 9, of which 4 were waited for; matrix products, arithmetic and copies ran while one was open for 1% of the time, Pallas kernels for 0%

profile of v2, /device:TPU:72, one launch (start us, length us, event | category | flops | bytes accessed | tf_op | source)
XLA Modules:
  0.0 121.8 jit_solution(11922138792600803465)
XLA Ops:
  0.6 0.8 copy.17
  1.4 0.6 pad_convert_fusion.params_ref
  2.0 4.2 %pack.1 = bf16[64,136,128]{2,1,0:T(8,128)(2,1)} custom-call(s32[64]{0:T(128)} %bitcast.60, f32[64,128]{1,0:T(8,128)} %pad_convert_fusion.params_ref, bf16[64,64,128]{2,1,0:T(8,128)(2,1)} %bitcast.56), custom_call_target="tpu_custom_call" | custom-call | tf_op jit(solution)/shard_map/pack/pallas_call | solution.py:69
  6.3 12.8 %all-to-all-start = ((bf16[64,136,128]{2,1,0:T(8,128)(2,1)}), bf16[64,136,128]{2,1,0:T(8,128)(2,1)S(1)}, u32[]{:S(2)}, u32[]{:S(2)}) async-start(bf16[64,136,128]{2,1,0:T(8,128)(2,1)} %pack.1), calls=%async_computation | async-start | bytes 4456448 | tf_op jit(solution)/shard_map/all_to_all | solution.py:157
  19.0 0.2 slice_reduce_fusion.3
  19.2 2.0 %collective-permute-start.1 = (f32[64]{0:T(128)S(1)}, f32[64]{0:T(128)S(1)}, u32[]{:S(2)}, u32[]{:S(2)}) collective-permute-start(f32[64]{0:T(128)S(1)} %get-tuple-element.5), channel_id=1, source_target_pairs={{0,8},{8,16},{16,24},{24,32},{32,40},{40,48},{48,56},{64,72},{72,8... | collective-permute-start | bytes 776 | tf_op jit(solution)/shard_map/ppermute | solution.py:25
  21.2 3.5 %collective-permute-start = (f32[64]{0:T(128)S(1)}, f32[64]{0:T(128)S(1)}, u32[]{:S(2)}, u32[]{:S(2)}) collective-permute-start(f32[64]{0:T(128)S(1)} %get-tuple-element.4), channel_id=1, source_target_pairs={{8,0},{16,8},{24,16},{32,24},{40,32},{48,40},{56,48},{72,64},{80,7... | collective-permute-start | bytes 776 | tf_op jit(solution)/shard_map/ppermute | solution.py:25
  24.8 2.5 %collective-permute-start.2 = (f32[128]{0:T(128)S(1)}, f32[128]{0:T(128)S(1)}, u32[]{:S(2)}, u32[]{:S(2)}) collective-permute-start(f32[128]{0:T(128)S(1)} %get-tuple-element.18), channel_id=1, source_target_pairs={{64,0},{72,8},{80,16},{88,24},{96,32},{104,40},{112,48},{120,56},{... | collective-permute-start | bytes 1544 | tf_op jit(solution)/shard_map/ppermute | solution.py:25
  27.3 3.4 %collective-permute-start.3 = (f32[128]{0:T(128)S(1)}, f32[128]{0:T(128)S(1)}, u32[]{:S(2)}, u32[]{:S(2)}) collective-permute-start(f32[128]{0:T(128)S(1)} %get-tuple-element.19), channel_id=1, source_target_pairs={{0,64},{8,72},{16,80},{24,88},{32,96},{40,104},{48,112},{56,120},{... | collective-permute-start | bytes 1544 | tf_op jit(solution)/shard_map/ppermute | solution.py:25
  30.7 24.9 %collective-permute-done.1 = f32[64]{0:T(128)S(1)} collective-permute-done((f32[64]{0:T(128)S(1)}, f32[64]{0:T(128)S(1)}, u32[]{:S(2)}, u32[]{:S(2)}) %collective-permute-start.1) | collective-permute-done | bytes 288 | tf_op jit(solution)/shard_map/ppermute | solution.py:25
  55.6 0.1 copy.19
  55.7 0.1 copy.18
  55.8 11.3 %collective-permute-done.2 = f32[128]{0:T(128)S(1)} collective-permute-done((f32[128]{0:T(128)S(1)}, f32[128]{0:T(128)S(1)}, u32[]{:S(2)}, u32[]{:S(2)}) %collective-permute-start.2) | collective-permute-done | bytes 544 | tf_op jit(solution)/shard_map/ppermute | solution.py:25
  67.2 0.1 fusion.10
  67.3 0.7 pad_maximum_fusion.refs_1_
  68.0 4.3 %all-to-all-done.refs_2_ = bf16[64,136,128]{2,1,0:T(8,128)(2,1)S(1)} async-done(((bf16[64,136,128]{2,1,0:T(8,128)(2,1)}), bf16[64,136,128]{2,1,0:T(8,128)(2,1)S(1)}, u32[]{:S(2)}, u32[]{:S(2)}) %all-to-all-start) | async-done | bytes 2228256 | tf_op jit(solution)/shard_map/all_to_all | solution.py:157
  72.3 0.8 reshape.31.refs_0_
  73.2 0.5 copy-done
  73.6 11.8 %terms.1 = f32[3,64,128]{2,1,0:T(8,128)} custom-call(f32[1024]{0:T(1024)} %reshape.31.refs_0_, f32[4,64,128]{2,1,0:T(8,128)} %pad_maximum_fusion.refs_1_, bf16[64,136,128]{2,1,0:T(8,128)(2,1)} %copy-done), custom_call_target="tpu_custom_call" | custom-call | tf_op jit(solution)/shard_map/terms/pallas_call | solution.py:171
  85.4 0.8 slice_bitcast_fusion.2
  86.2 0.7 slice_bitcast_fusion.3
  86.9 0.2 slice_reduce_fusion
  87.0 2.3 %collective-permute-start.5 = (f32[64]{0:T(128)S(1)}, f32[64]{0:T(128)S(1)}, u32[]{:S(2)}, u32[]{:S(2)}) collective-permute-start(f32[64]{0:T(128)S(1)} %get-tuple-element.3), channel_id=1, source_target_pairs={{8,0},{16,8},{24,16},{32,24},{40,32},{48,40},{56,48},{72,64},{80,7... | collective-permute-start | bytes 776 | tf_op jit(solution)/shard_map/ppermute | solution.py:25
  89.4 1.9 %collective-permute-start.6 = (f32[128]{0:T(128)S(1)}, f32[128]{0:T(128)S(1)}, u32[]{:S(2)}, u32[]{:S(2)}) collective-permute-start(f32[128]{0:T(128)S(1)} %get-tuple-element.11), channel_id=1, source_target_pairs={{0,64},{8,72},{16,80},{24,88},{32,96},{40,104},{48,112},{56,120},{... | collective-permute-start | bytes 1544 | tf_op jit(solution)/shard_map/ppermute | solution.py:25
  91.3 3.9 %collective-permute-start.7 = (f32[128]{0:T(128)S(1)}, f32[128]{0:T(128)S(1)}, u32[]{:S(2)}, u32[]{:S(2)}) collective-permute-start(f32[128]{0:T(128)S(1)} %get-tuple-element.12), channel_id=1, source_target_pairs={{64,0},{72,8},{80,16},{88,24},{96,32},{104,40},{112,48},{120,56},{... | collective-permute-start | bytes 1544 | tf_op jit(solution)/shard_map/ppermute | solution.py:25
  95.2 1.9 %collective-permute-start.4 = (f32[64]{0:T(128)S(1)}, f32[64]{0:T(128)S(1)}, u32[]{:S(2)}, u32[]{:S(2)}) collective-permute-start(f32[64]{0:T(128)S(1)} %get-tuple-element.2), channel_id=1, source_target_pairs={{0,8},{8,16},{16,24},{24,32},{32,40},{40,48},{48,56},{64,72},{72,8... | collective-permute-start | bytes 776 | tf_op jit(solution)/shard_map/ppermute | solution.py:25
  97.2 2.9 %collective-permute-done.4 = f32[64]{0:T(128)S(1)} collective-permute-done((f32[64]{0:T(128)S(1)}, f32[64]{0:T(128)S(1)}, u32[]{:S(2)}, u32[]{:S(2)}) %collective-permute-start.4) | collective-permute-done | bytes 288 | tf_op jit(solution)/shard_map/ppermute | solution.py:25
  100.1 0.1 copy.21
  100.2 0.1 copy.20
  100.3 0.7 fusion.17
  101.1 20.1 %all_to_all.10 = f32[8,2,8,128]{3,2,1,0:T(8,128)S(1)} all-to-all(f32[8,2,8,128]{3,2,1,0:T(8,128)S(1)} %maximum_bitcast_fusion), channel_id=1, replica_groups=mesh['tile'=64,'img'=8] {'img'}, dimensions={0} | all-to-all | bytes 131072 | tf_op jit(solution)/shard_map/all_to_all | solution.py:191
  121.2 0.6 fusion.19
  (20 shorter events, 0.2 us)
Async XLA Ops:
  6.3 12.8 %copy-start.1 = (f32[1,64,128]{2,1,0:T(8,128)S(1)}, f32[1,64,128]{2,1,0:T(8,128)}, u32[]{:S(2)}) copy-start(f32[1,64,128]{2,1,0:T(8,128)} %param.5) | copy-start | bytes 98308
  6.3 61.0 %copy-start.2 = (f32[1,64,128]{2,1,0:T(8,128)S(1)}, f32[1,64,128]{2,1,0:T(8,128)}, u32[]{:S(2)}) copy-start(f32[1,64,128]{2,1,0:T(8,128)} %param.6) | copy-start | bytes 98308
  6.3 66.0 %all-to-all-start = ((bf16[64,136,128]{2,1,0:T(8,128)(2,1)}), bf16[64,136,128]{2,1,0:T(8,128)(2,1)S(1)}, u32[]{:S(2)}, u32[]{:S(2)}) async-start(bf16[64,136,128]{2,1,0:T(8,128)(2,1)} %pack.1), calls=%async_computation | async-start | bytes 4456448 | tf_op jit(solution)/shard_map/all_to_all | solution.py:157
  19.2 36.4 %collective-permute-start.1 = (f32[64]{0:T(128)S(1)}, f32[64]{0:T(128)S(1)}, u32[]{:S(2)}, u32[]{:S(2)}) collective-permute-start(f32[64]{0:T(128)S(1)} %get-tuple-element.5), channel_id=1, source_target_pairs={{0,8},{8,16},{16,24},{24,32},{32,40},{40,48},{48,56},{64,72},{72,8... | collective-permute-start | bytes 776 | tf_op jit(solution)/shard_map/ppermute | solution.py:25
  21.2 34.4 %collective-permute-start = (f32[64]{0:T(128)S(1)}, f32[64]{0:T(128)S(1)}, u32[]{:S(2)}, u32[]{:S(2)}) collective-permute-start(f32[64]{0:T(128)S(1)} %get-tuple-element.4), channel_id=1, source_target_pairs={{8,0},{16,8},{24,16},{32,24},{40,32},{48,40},{56,48},{72,64},{80,7... | collective-permute-start | bytes 776 | tf_op jit(solution)/shard_map/ppermute | solution.py:25
  24.8 42.4 %collective-permute-start.2 = (f32[128]{0:T(128)S(1)}, f32[128]{0:T(128)S(1)}, u32[]{:S(2)}, u32[]{:S(2)}) collective-permute-start(f32[128]{0:T(128)S(1)} %get-tuple-element.18), channel_id=1, source_target_pairs={{64,0},{72,8},{80,16},{88,24},{96,32},{104,40},{112,48},{120,56},{... | collective-permute-start | bytes 1544 | tf_op jit(solution)/shard_map/ppermute | solution.py:25
  27.3 39.9 %collective-permute-start.3 = (f32[128]{0:T(128)S(1)}, f32[128]{0:T(128)S(1)}, u32[]{:S(2)}, u32[]{:S(2)}) collective-permute-start(f32[128]{0:T(128)S(1)} %get-tuple-element.19), channel_id=1, source_target_pairs={{0,64},{8,72},{16,80},{24,88},{32,96},{40,104},{48,112},{56,120},{... | collective-permute-start | bytes 1544 | tf_op jit(solution)/shard_map/ppermute | solution.py:25
  72.2 1.4 %copy-start = (bf16[64,136,128]{2,1,0:T(8,128)(2,1)}, bf16[64,136,128]{2,1,0:T(8,128)(2,1)S(1)}, u32[]{:S(2)}) copy-start(bf16[64,136,128]{2,1,0:T(8,128)(2,1)S(1)} %all-to-all-done.refs_2_) | copy-start | bytes 6684676
  87.0 10.1 %collective-permute-start.5 = (f32[64]{0:T(128)S(1)}, f32[64]{0:T(128)S(1)}, u32[]{:S(2)}, u32[]{:S(2)}) collective-permute-start(f32[64]{0:T(128)S(1)} %get-tuple-element.3), channel_id=1, source_target_pairs={{8,0},{16,8},{24,16},{32,24},{40,32},{48,40},{56,48},{72,64},{80,7... | collective-permute-start | bytes 776 | tf_op jit(solution)/shard_map/ppermute | solution.py:25
  89.4 10.9 %collective-permute-start.6 = (f32[128]{0:T(128)S(1)}, f32[128]{0:T(128)S(1)}, u32[]{:S(2)}, u32[]{:S(2)}) collective-permute-start(f32[128]{0:T(128)S(1)} %get-tuple-element.11), channel_id=1, source_target_pairs={{0,64},{8,72},{16,80},{24,88},{32,96},{40,104},{48,112},{56,120},{... | collective-permute-start | bytes 1544 | tf_op jit(solution)/shard_map/ppermute | solution.py:25
  91.3 9.0 %collective-permute-start.7 = (f32[128]{0:T(128)S(1)}, f32[128]{0:T(128)S(1)}, u32[]{:S(2)}, u32[]{:S(2)}) collective-permute-start(f32[128]{0:T(128)S(1)} %get-tuple-element.12), channel_id=1, source_target_pairs={{64,0},{72,8},{80,16},{88,24},{96,32},{104,40},{112,48},{120,56},{... | collective-permute-start | bytes 1544 | tf_op jit(solution)/shard_map/ppermute | solution.py:25
  95.2 4.9 %collective-permute-start.4 = (f32[64]{0:T(128)S(1)}, f32[64]{0:T(128)S(1)}, u32[]{:S(2)}, u32[]{:S(2)}) collective-permute-start(f32[64]{0:T(128)S(1)} %get-tuple-element.2), channel_id=1, source_target_pairs={{0,8},{8,16},{16,24},{24,32},{32,40},{40,48},{48,56},{64,72},{72,8... | collective-permute-start | bytes 776 | tf_op jit(solution)/shard_map/ppermute | solution.py:25
